TPU v7x, 32 devices: a whole 2x2x4 slice. The times are simulated.
32 devices in a mesh: dp: 16 (over z, x, core), ep: 2 (over y).
Axes of the slice: x: 2, y: 2, z: 4, core: 2. Of those that a mesh axis runs over, the one named last changes fastest.
Arguments:
- query_rows: bfloat16 [32, 128, 576], P(('dp', 'ep')), may hold values from -65 to 65, as said below
- cache_latent: bfloat16 [131072, 576], P(('dp', 'ep')), may hold values from -6 to 6, as said below
- lengths: int32 [32], replicated, may hold values from 2 to 4096, as said below
- moe_input: bfloat16 [256, 7168], P(('dp', 'ep')), may hold values from -6 to 6
- expert_ids: int32 [256, 8], P(('dp', 'ep')), may hold values from 0 to 15, all different within a row; in each aligned block of 8 rows (0 to 7, 8 to 15, ...) at most 4 rows name the same one
- gate_weights: float32 [256, 8], P(('dp', 'ep')), may hold values from 0.05 to 0.5
- expert_gate: bfloat16 [16, 7168, 1024], P('dp', None, 'ep'), may hold values from -0.0625 to 0.0625
- expert_up: bfloat16 [16, 7168, 1024], P('dp', None, 'ep'), may hold values from -0.0625 to 0.0625
- expert_down: bfloat16 [16, 1024, 7168], P('dp', 'ep'), may hold values from -0.1875 to 0.1875
Outputs:
- attn_out: bfloat16 [32, 128, 512], P(('dp', 'ep'))
- moe_out: bfloat16 [256, 7168], P(('dp', 'ep'))
Inputs may be any that keep to these rules, and one draw needn't show every extreme that they name: `lengths`: some request has exactly 4096 cached tokens in every draw. `expert_ids`: each row names 8 different experts. Among the rows of one device no expert is named more than 4 times, a bound that some block reaches. `cache_latent`: finite latent entries. `query_rows`: finite query entries.
All inputs are finite; a program needn't handle non-finite values.
Results may differ from a plain program's by a relative error of at most 0.008.
Values may be sent and summed in bfloat16 or wider, within the bound.
A program may use at most 128 MiB of HBM per device.

v0:
```python
import jax
import jax.numpy as jnp
from jax import lax
from jax.sharding import PartitionSpec as P

WIDTH = 7168
LATENT = 512
TOPK = 8


qk_scale = 192.0 ** (-0.5)
far_low = -1e30
attend_rows = 512


def partial_attend(query_row, key_rows, live_mask):
    scores = qk_scale * lax.dot_general(
        query_row, key_rows, (((1,), (1,)), ((), ())), preferred_element_type=jnp.float32
    )
    scores = jnp.where(live_mask[None, :], scores, far_low)
    score_top = jnp.max(scores, axis=1)
    exponent = jnp.where(live_mask[None, :], jnp.exp(scores - score_top[:, None]), 0.0)
    weight_sum = jnp.sum(exponent, axis=1)
    mixed_values = jnp.dot(
        exponent.astype(jnp.bfloat16), key_rows[:, :LATENT], preferred_element_type=jnp.float32
    )
    return (score_top, weight_sum, mixed_values)


def merge_parts(first, second):
    top_first, sum_first, mix_first = first
    top_second, sum_second, mix_second = second
    score_top = jnp.maximum(top_first, top_second)
    scale_first = jnp.exp(top_first - score_top)
    scale_second = jnp.exp(top_second - score_top)
    return (
        score_top,
        sum_first * scale_first + sum_second * scale_second,
        mix_first * scale_first[:, None] + mix_second * scale_second[:, None],
    )


def local_attend(query_row, cache_rows, keep_end):
    head_count = query_row.shape[0]
    block_total = (keep_end + attend_rows - 1) // attend_rows
    initial = (
        jnp.full((head_count,), far_low, jnp.float32),
        jnp.zeros((head_count,), jnp.float32),
        jnp.zeros((head_count, LATENT), jnp.float32),
    )

    def block_step(block_index, carry):
        start_row = block_index * attend_rows
        key_rows = lax.dynamic_slice_in_dim(cache_rows, start_row, attend_rows, 0)
        live_mask = start_row + jnp.arange(attend_rows, dtype=jnp.int32) < keep_end
        return merge_parts(carry, partial_attend(query_row, key_rows, live_mask))

    return lax.fori_loop(0, block_total, block_step, initial)


def per_device(
    query_rows,
    cache_latent,
    lengths,
    moe_input,
    expert_ids,
    gate_weights,
    expert_gate,
    expert_up,
    expert_down,
):
    ranks_dp = lax.axis_size("dp")
    ranks_ep = lax.axis_size("ep")
    here_dp = lax.axis_index("dp")
    here_ep = lax.axis_index("ep")
    own_rank = here_dp * ranks_ep + here_ep
    own_length = lengths[own_rank]
    query_row = query_rows[0]
    score_top, weight_sum, mixed_values = local_attend(query_row, cache_latent, own_length)
    attn_out = (mixed_values / weight_sum[:, None]).astype(jnp.bfloat16)[None]
    tok_count = moe_input.shape[0]
    slot_count = tok_count * TOPK
    capacity = max(tok_count // 2, tok_count * TOPK // ranks_dp)
    flat_ids = expert_ids.reshape(slot_count)
    onehot = (flat_ids[:, None] == jnp.arange(ranks_dp, dtype=jnp.int32)[None, :]).astype(jnp.int32)
    before = jnp.cumsum(onehot, axis=0) - onehot
    position = jnp.sum(before * onehot, axis=1)
    slot_index = flat_ids * capacity + position
    row_numbers = jnp.arange(ranks_dp * capacity, dtype=jnp.int32)
    dispatch_table = jnp.any(
        row_numbers[:, None, None] == slot_index.reshape(tok_count, TOPK)[None], axis=2
    ).astype(jnp.bfloat16)
    packed = jnp.dot(dispatch_table, moe_input, preferred_element_type=jnp.float32).astype(
        jnp.bfloat16
    )
    packed = packed.reshape(ranks_dp, capacity, WIDTH)
    gate_proj = expert_gate[0]
    up_proj = expert_up[0]
    down_proj = expert_down[0]
    ranks_all = ranks_dp * ranks_ep
    spread = jnp.broadcast_to(packed[:, None], (ranks_dp, ranks_ep, capacity, WIDTH)).reshape(
        ranks_all, capacity, WIDTH
    )
    shard_rows = lax.all_to_all(spread, ("dp", "ep"), split_axis=0, concat_axis=0, tiled=True)
    item_count = shard_rows.shape[1]
    flat_rows = shard_rows.reshape(ranks_all * item_count, WIDTH)
    gate_act = jnp.dot(flat_rows, gate_proj, preferred_element_type=jnp.float32)
    up_act = jnp.dot(flat_rows, up_proj, preferred_element_type=jnp.float32)
    partial_sum = jnp.dot(
        (jax.nn.silu(gate_act) * up_act).astype(jnp.bfloat16),
        down_proj,
        preferred_element_type=jnp.float32,
    )
    partial_sum = partial_sum.astype(jnp.bfloat16).reshape(ranks_all, item_count, WIDTH)
    returned = lax.all_to_all(partial_sum, ("dp", "ep"), split_axis=0, concat_axis=0, tiled=True)
    grouped = returned.reshape(ranks_dp, ranks_ep, item_count, WIDTH)
    running_sum = grouped[:, 0].astype(jnp.float32)
    for group_number in range(1, ranks_ep):
        running_sum = running_sum + grouped[:, group_number].astype(jnp.float32)
    expert_out = running_sum.astype(jnp.bfloat16)
    gathered = expert_out.reshape(ranks_dp * capacity, WIDTH)[slot_index].reshape(
        tok_count, TOPK, WIDTH
    )
    moe_sum = jnp.einsum("tk,tkd->td", gate_weights, gathered.astype(jnp.float32))
    return (attn_out, moe_sum.astype(jnp.bfloat16))


def solution(mesh):
    placed = (
        P(("dp", "ep"), None, None),
        P(("dp", "ep"), None),
        P(),
        P(("dp", "ep"), None),
        P(("dp", "ep"), None),
        P(("dp", "ep"), None),
        P("dp", None, "ep"),
        P("dp", None, "ep"),
        P("dp", "ep", None),
    )
    return jax.shard_map(
        per_device,
        mesh=mesh,
        in_specs=placed,
        out_specs=(P(("dp", "ep"), None, None), P(("dp", "ep"), None)),
        check_vma=False,
    )
```

profile of v0, /device:TPU:0, one launch (start us, length us, event | category | flops | bytes accessed | tf_op | source)
XLA Modules:
  0.0 125.3 jit_solution(10674229525956903997)
XLA Ops:
  0.6 0.8 eq.29
  1.9 0.7 broadcast_multiply_fusion
  2.7 0.4 convolution_convert_fusion.1
  3.5 1.8 %broadcast_in_dim.53 = bf16[16,2,4,7168]{3,2,1,0:T(4,128)(2,1)} broadcast(bf16[16,4,7168]{2,1,0:T(4,128)(2,1)S(1)} %broadcast_in_dim.52), dimensions={0,2,3} | broadcast | bytes 2752512 | tf_op jit(solution)/shard_map/broadcast_in_dim | solution.py:101
  5.3 7.4 %all-to-all-start = ((bf16[32,4,7168]{2,1,0:T(4,128)(2,1)}), bf16[32,4,7168]{2,1,0:T(4,128)(2,1)}, u32[]{:S(2)}, u32[]{:S(2)}) async-start(bf16[32,4,7168]{2,1,0:T(4,128)(2,1)} %bitcast.3), calls=%async_computation | async-start | bytes 3670016 | tf_op jit(solution)/shard_map/all_to_all | solution.py:104
  12.7 0.6 dynamic_slice.6
  14.3 41.5 %all-to-all-done = bf16[32,4,7168]{2,1,0:T(4,128)(2,1)} async-done(((bf16[32,4,7168]{2,1,0:T(4,128)(2,1)}), bf16[32,4,7168]{2,1,0:T(4,128)(2,1)}, u32[]{:S(2)}, u32[]{:S(2)}) %all-to-all-start) | async-done | bytes 1835040 | tf_op jit(solution)/shard_map/all_to_all | solution.py:104
  55.8 2.9 %reshape.73 = bf16[128,7168]{1,0:T(8,128)(2,1)S(1)} reshape(bf16[32,4,7168]{2,1,0:T(4,128)(2,1)} %all-to-all-done) | data formatting | bytes 3670016 | tf_op jit(solution)/shard_map/reshape | solution.py:106
  58.7 4.2 %fusion.16 = f32[128,512]{1,0:T(8,128)S(1)} fusion(bf16[128,7168]{1,0:T(8,128)(2,1)S(1)} %reshape.73, bf16[1,7168,512]{2,1,0:T(8,128)(2,1)} %param.17), kind=kOutput, calls=%fused_computation.25 | convolution fusion | flops 939524096 | bytes 9437184 | tf_op jit(solution)/shard_map/dot_general | solution.py:107
  62.9 8.6 %convolution_convert_fusion = bf16[128,7168]{1,0:T(8,128)(2,1)} fusion(bf16[1,512,7168]{2,1,0:T(8,128)(2,1)} %param.19, bf16[128,7168]{1,0:T(8,128)(2,1)S(1)} %reshape.73, bf16[1,7168,512]{2,1,0:T(8,128)(2,1)} %param.18, f32[128,512]{1,0:T(8,128)S(1)} %fusion.16), kind=kOutput, calls=%fused_computation.20 | convolution fusion | flops 1880358912 | bytes 18612224 | tf_op jit(solution)/shard_map/dot_general | solution.py:109
  71.5 4.1 %reshape.74 = bf16[32,4,7168]{2,1,0:T(4,128)(2,1)} reshape(bf16[128,7168]{1,0:T(8,128)(2,1)} %convolution_convert_fusion) | data formatting | bytes 3670016 | tf_op jit(solution)/shard_map/reshape | solution.py:114
  75.6 3.6 %all-to-all-start.1 = ((bf16[32,4,7168]{2,1,0:T(4,128)(2,1)}), bf16[32,4,7168]{2,1,0:T(4,128)(2,1)S(1)}, u32[]{:S(2)}, u32[]{:S(2)}) async-start(bf16[32,4,7168]{2,1,0:T(4,128)(2,1)} %reshape.74), calls=%async_computation.1 | async-start | bytes 3670016 | tf_op jit(solution)/shard_map/all_to_all | solution.py:115
  79.3 7.7 %while.14 = (s32[]{:T(128)}, f32[128]{0:T(128)S(1)}, f32[128]{0:T(128)S(1)}, f32[128,512]{1,0:T(8,128)S(1)}, s32[]{:T(128)}, /*index=5*/s32[]{:T(128)}, bf16[409...) while((s32[]{:T(128)}, f32[128]{0:T(128)S(1)}, ...), condition=%wide.region_3.4_spmd, body=%wide.region_0.3_spmd.sunk | while | flops 143394304 | bytes 2581683 | solution.py:58
  79.4 0.7 add_compare_fusion.2
  80.0 1.5 %fusion.56 = (f32[128]{0:T(128)S(1)}, f32[512,128]{1,0:T(8,128)S(1)}) fusion(bf16[128,576]{1,0:T(8,128)(2,1)S(1)} %get-tuple-element.165, bf16[4096,576]{0,1:T(8,128)(2,1)} %get-tuple-element.164, s32[]{:T(128)S(6)} %select_n.48, pred[512]{0:T(512)(128)(4,1)S(1)} %add_compare_fusion.2), kind=kOutput, calls=%fused_computation.55.clone.1 | convolution fusion | flops 75693952 | bytes 1000452 | tf_op jit(solution)/shard_map/while/body/dot_general | solution.py:17
  81.7 1.5 %fusion.58 = f32[128,512]{1,0:T(8,128)S(1)} fusion(bf16[4096,576]{0,1:T(8,128)(2,1)} %get-tuple-element.164, s32[]{:T(128)S(6)} %select_n.48, f32[128,512]{1,0:T(8,128)S(1)} %get-tuple-element.149, f32[512,128]{1,0:T(8,128)S(1)} %get-tuple-element.128, f32[128]{0:T(128)S(1)} %get-tuple-element.132, f32[128]{0:T(128)S(1)} %get-tuple-element.133, ...), kind=kOutput, calls=%fused_computation.3.clone.1 | convolution fusion | flops 67502080 | bytes 1312772 | tf_op jit(solution)/shard_map/while/body/dot_general | solution.py:24
  83.2 0.7 add_compare_fusion.2
  83.9 1.5 %fusion.56 = (f32[128]{0:T(128)S(1)}, f32[512,128]{1,0:T(8,128)S(1)}) fusion(bf16[128,576]{1,0:T(8,128)(2,1)S(1)} %get-tuple-element.165, bf16[4096,576]{0,1:T(8,128)(2,1)} %get-tuple-element.164, s32[]{:T(128)S(6)} %select_n.48, pred[512]{0:T(512)(128)(4,1)S(1)} %add_compare_fusion.2), kind=kOutput, calls=%fused_computation.55.clone.1 | convolution fusion | flops 75693952 | bytes 1000452 | tf_op jit(solution)/shard_map/while/body/dot_general | solution.py:17
  85.5 1.5 %fusion.58 = f32[128,512]{1,0:T(8,128)S(1)} fusion(bf16[4096,576]{0,1:T(8,128)(2,1)} %get-tuple-element.164, s32[]{:T(128)S(6)} %select_n.48, f32[128,512]{1,0:T(8,128)S(1)} %get-tuple-element.149, f32[512,128]{1,0:T(8,128)S(1)} %get-tuple-element.128, f32[128]{0:T(128)S(1)} %get-tuple-element.132, f32[128]{0:T(128)S(1)} %get-tuple-element.133, ...), kind=kOutput, calls=%fused_computation.3.clone.1 | convolution fusion | flops 67502080 | bytes 1312772 | tf_op jit(solution)/shard_map/while/body/dot_general | solution.py:24
  87.1 0.7 fusion.34
  87.8 34.5 %all-to-all-done.1 = bf16[32,4,7168]{2,1,0:T(4,128)(2,1)S(1)} async-done(((bf16[32,4,7168]{2,1,0:T(4,128)(2,1)}), bf16[32,4,7168]{2,1,0:T(4,128)(2,1)S(1)}, u32[]{:S(2)}, u32[]{:S(2)}) %all-to-all-start.1) | async-done | bytes 1835040 | tf_op jit(solution)/shard_map/all_to_all | solution.py:115
  122.4 0.5 add_convert_fusion
  123.1 1.1 gather_fusion
  124.6 0.7 copy.22
  (27 shorter events, 2.1 us)
Async XLA Ops:
  0.6 2.1 %copy-start = (bf16[8,7168]{1,0:T(8,128)(2,1)S(1)}, bf16[8,7168]{1,0:T(8,128)(2,1)}, u32[]{:S(2)}) copy-start(bf16[8,7168]{1,0:T(8,128)(2,1)} %param.14) | copy-start | bytes 344068
  3.5 9.2 %copy-start.3 = (s32[32]{0:T(128)S(1)}, s32[32]{0:T(128)}, u32[]{:S(2)}) copy-start(s32[32]{0:T(128)} %param.13) | copy-start | bytes 388
  3.5 10.6 %copy-start.1 = (bf16[1,128,576]{1,2,0:T(8,128)(2,1)S(1)}, bf16[1,128,576]{1,2,0:T(8,128)(2,1)}, u32[]{:S(2)}) copy-start(bf16[1,128,576]{1,2,0:T(8,128)(2,1)} %param.11) | copy-start | bytes 442372
  5.3 50.5 %all-to-all-start = ((bf16[32,4,7168]{2,1,0:T(4,128)(2,1)}), bf16[32,4,7168]{2,1,0:T(4,128)(2,1)}, u32[]{:S(2)}, u32[]{:S(2)}) async-start(bf16[32,4,7168]{2,1,0:T(4,128)(2,1)} %bitcast.3), calls=%async_computation | async-start | bytes 3670016 | tf_op jit(solution)/shard_map/all_to_all | solution.py:104
  75.6 46.7 %all-to-all-start.1 = ((bf16[32,4,7168]{2,1,0:T(4,128)(2,1)}), bf16[32,4,7168]{2,1,0:T(4,128)(2,1)S(1)}, u32[]{:S(2)}, u32[]{:S(2)}) async-start(bf16[32,4,7168]{2,1,0:T(4,128)(2,1)} %reshape.74), calls=%async_computation.1 | async-start | bytes 3670016 | tf_op jit(solution)/shard_map/all_to_all | solution.py:115
  123.0 1.1 copy-start.2
where the time goes:
time: 127 us; the launch traced here: 125 us
  waiting for transfers between devices  76 us (60%)
  matrix products  19.6 us (15%)
  local copies, waits for them, and re-layouts  12.9 us (10%)
  starting transfers between devices  11.1 us (9%)
  other arithmetic  4.05 us (3%)
  between operations  1.5 us (1%)
    all_to_all x1, waiting for transfers between devices, per_device(): lax.all_to_all(spread, ('dp', 'ep'), split_axis=0, concat_axis=0, tiled=T...  41.5 us
    all_to_all x1, waiting for transfers between devices, per_device(): lax.all_to_all(partial_sum, ('dp', 'ep'), split_axis=0, concat_axis=0, ti...  34.5 us
    dot_general x1, matrix products, per_device(): jnp.dot((jax.nn.silu(gate_act) * up_act).astype(jnp.bfloat16), down_proj,...  8.61 us
    all_to_all x1, starting transfers between devices, per_device(): lax.all_to_all(spread, ('dp', 'ep'), split_axis=0, concat_axis=0, tiled=T...  7.44 us
    dot_general x1, matrix products, per_device(): gate_act = jnp.dot(flat_rows, gate_proj, preferred_element_type=jnp.float32)  4.2 us
    reshape x1, local copies, waits for them, and re-layouts, per_device(): partial_sum.astype(jnp.bfloat16).reshape(ranks_all, item_count, WIDTH)  4.1 us
    all_to_all x1, starting transfers between devices, per_device(): lax.all_to_all(partial_sum, ('dp', 'ep'), split_axis=0, concat_axis=0, ti...  3.65 us
    dot_general x2, matrix products, partial_attend(): jnp.dot(exponent.astype(jnp.bfloat16), key_rows[:, :LATENT], preferred_el...  3.04 us
  transfers between devices with their start and end apart: 2, of which 2 were waited for; matrix products, arithmetic and copies ran while one was open for 7% of the time, Pallas kernels for 0%

commit v1 on v0

--- a/solution.py
+++ b/solution.py
@@ -78,50 +78,17 @@
     query_row = query_rows[0]
     score_top, weight_sum, mixed_values = local_attend(query_row, cache_latent, own_length)
     attn_out = (mixed_values / weight_sum[:, None]).astype(jnp.bfloat16)[None]
-    tok_count = moe_input.shape[0]
-    slot_count = tok_count * TOPK
-    capacity = max(tok_count // 2, tok_count * TOPK // ranks_dp)
-    flat_ids = expert_ids.reshape(slot_count)
-    onehot = (flat_ids[:, None] == jnp.arange(ranks_dp, dtype=jnp.int32)[None, :]).astype(jnp.int32)
-    before = jnp.cumsum(onehot, axis=0) - onehot
-    position = jnp.sum(before * onehot, axis=1)
-    slot_index = flat_ids * capacity + position
-    row_numbers = jnp.arange(ranks_dp * capacity, dtype=jnp.int32)
-    dispatch_table = jnp.any(
-        row_numbers[:, None, None] == slot_index.reshape(tok_count, TOPK)[None], axis=2
-    ).astype(jnp.bfloat16)
-    packed = jnp.dot(dispatch_table, moe_input, preferred_element_type=jnp.float32).astype(
-        jnp.bfloat16
-    )
-    packed = packed.reshape(ranks_dp, capacity, WIDTH)
-    gate_proj = expert_gate[0]
-    up_proj = expert_up[0]
-    down_proj = expert_down[0]
-    ranks_all = ranks_dp * ranks_ep
-    spread = jnp.broadcast_to(packed[:, None], (ranks_dp, ranks_ep, capacity, WIDTH)).reshape(
-        ranks_all, capacity, WIDTH
-    )
-    shard_rows = lax.all_to_all(spread, ("dp", "ep"), split_axis=0, concat_axis=0, tiled=True)
-    item_count = shard_rows.shape[1]
-    flat_rows = shard_rows.reshape(ranks_all * item_count, WIDTH)
-    gate_act = jnp.dot(flat_rows, gate_proj, preferred_element_type=jnp.float32)
-    up_act = jnp.dot(flat_rows, up_proj, preferred_element_type=jnp.float32)
-    partial_sum = jnp.dot(
-        (jax.nn.silu(gate_act) * up_act).astype(jnp.bfloat16),
-        down_proj,
-        preferred_element_type=jnp.float32,
-    )
-    partial_sum = partial_sum.astype(jnp.bfloat16).reshape(ranks_all, item_count, WIDTH)
-    returned = lax.all_to_all(partial_sum, ("dp", "ep"), split_axis=0, concat_axis=0, tiled=True)
-    grouped = returned.reshape(ranks_dp, ranks_ep, item_count, WIDTH)
-    running_sum = grouped[:, 0].astype(jnp.float32)
-    for group_number in range(1, ranks_ep):
-        running_sum = running_sum + grouped[:, group_number].astype(jnp.float32)
-    expert_out = running_sum.astype(jnp.bfloat16)
-    gathered = expert_out.reshape(ranks_dp * capacity, WIDTH)[slot_index].reshape(
-        tok_count, TOPK, WIDTH
-    )
-    moe_sum = jnp.einsum("tk,tkd->td", gate_weights, gathered.astype(jnp.float32))
+    axes = ("dp", "ep")
+    all_rows = lax.all_gather(moe_input, axes, axis=0, tiled=True)
+    all_ids = lax.all_gather(expert_ids, axes, axis=0, tiled=True)
+    all_weights = lax.all_gather(gate_weights, axes, axis=0, tiled=True)
+    row_weight = jnp.sum(jnp.where(all_ids == here_dp, all_weights, 0.0), axis=1, keepdims=True)
+    gate_act = jnp.dot(all_rows, expert_gate[0], preferred_element_type=jnp.float32)
+    up_act = jnp.dot(all_rows, expert_up[0], preferred_element_type=jnp.float32)
+    hidden = (jax.nn.silu(gate_act) * up_act).astype(jnp.bfloat16)
+    partial_sum = jnp.dot(hidden, expert_down[0], preferred_element_type=jnp.float32)
+    weighted = (partial_sum * row_weight).astype(jnp.bfloat16)
+    moe_sum = lax.psum_scatter(weighted, axes, scatter_dimension=0, tiled=True)
     return (attn_out, moe_sum.astype(jnp.bfloat16))
 
 

time: 127 us -> 310 us (2.44)
  blocking collectives: 0 us -> 135 us
  waiting for transfers between devices: 76 us -> 135 us
  between operations: 1.5 us -> 14.7 us
  local copies, waits for them, and re-layouts: 12.9 us -> 0.79 us
  starting transfers between devices: 11.1 us -> 0.08 us
    all_gather x0 -> x2, blocking collectives: none -> 135 us  [the longest x1 70.9 us: per_device(): all_ids = lax.all_gather(expert_ids, axes, axis=0, tiled=True)]
    reduce_scatter x0 -> x1, waiting for transfers between devices: none -> 134 us  [per_device(): moe_sum = lax.psum_scatter(weighted, axes, scatter_dimension=0, tiled=True)]
    all_to_all x2 -> x0, waiting for transfers between devices: 76 us -> none  [the longest x1 41.5 us: per_device(): lax.all_to_all(spread, ('dp', 'ep'), split_axis=0, concat_axis=0, tiled=T...]
    all_to_all x2 -> x0, starting transfers between devices: 11.1 us -> none  [the longest x1 7.44 us: per_device(): lax.all_to_all(spread, ('dp', 'ep'), split_axis=0, concat_axis=0, tiled=T...]
    reshape x2 -> x0, local copies, waits for them, and re-layouts: 7.04 us -> none  [the longest x1 4.1 us: per_device(): partial_sum.astype(jnp.bfloat16).reshape(ranks_all, item_count, WIDTH)]
    dot_general x4 -> x2, matrix products: 13.6 us -> 18.4 us  [the longest x1 12.1 us: per_device(): jnp.dot(hidden, expert_down[0], preferred_element_type=jnp.float32)]
  transfers between devices with their start and end apart: 2 -> 2, of which waited for: 2 -> 1; matrix products, arithmetic and copies ran while one was open for 7% -> 2% of each run, Pallas kernels for 0% -> 0%
where the time goes in v1:
time: 310 us; the launch traced here: 309 us
  waiting for transfers between devices  135 us (44%)
  blocking collectives  135 us (44%)
  matrix products  21.3 us (7%)
  between operations  14.7 us (5%)
    reduce_scatter x1, waiting for transfers between devices, per_device(): moe_sum = lax.psum_scatter(weighted, axes, scatter_dimension=0, tiled=True)  134 us
    all_gather x1, blocking collectives, per_device(): all_ids = lax.all_gather(expert_ids, axes, axis=0, tiled=True)  70.9 us
    all_gather x1, blocking collectives, per_device(): all_weights = lax.all_gather(gate_weights, axes, axis=0, tiled=True)  64.3 us
    dot_general x1, matrix products, per_device(): jnp.dot(hidden, expert_down[0], preferred_element_type=jnp.float32)  12.1 us
    dot_general x1, matrix products, per_device(): jnp.dot(all_rows, expert_gate[0], preferred_element_type=jnp.float32)  6.25 us
  transfers between devices with their start and end apart: 2, of which 1 were waited for; matrix products, arithmetic and copies ran while one was open for 2% of the time, Pallas kernels for 0%

profile of v1, /device:TPU:0, one launch (start us, length us, event | category | flops | bytes accessed | tf_op | source)
XLA Modules:
  0.0 308.7 jit_solution(15779578487523013445)
XLA Ops:
  7.2 0.0 all-gather.2.cloned.1.call-start
  7.2 0.7 all-gather.2.cloned.1.call-update
  7.9 0.0 reduce-scatter.2.cloned.1.call-start
  7.9 70.9 %all_gather.10 = s32[256,8]{1,0:T(8,128)S(1)} all-gather(s32[8,8]{1,0:T(8,128)} %param.15), channel_id=1, replica_groups=mesh['dp'=16,'ep'=2] {'dp','ep'}, dimensions={0}, use_global_device_ids=true | all-gather | bytes 8448 | tf_op jit(solution)/shard_map/all_gather | solution.py:83
  78.8 64.3 %all_gather.11 = f32[256,8]{1,0:T(8,128)S(1)} all-gather(f32[8,8]{1,0:T(8,128)} %param.16), channel_id=1, replica_groups=mesh['dp'=16,'ep'=2] {'dp','ep'}, dimensions={0}, use_global_device_ids=true | all-gather | bytes 8448 | tf_op jit(solution)/shard_map/all_gather | solution.py:84
  143.1 0.1 select_reduce_fusion
  143.2 0.0 all-gather.2.cloned.1.call-done
  143.3 6.2 %fusion.17 = f32[256,512]{1,0:T(8,128)S(1)} fusion(bf16[256,7168]{1,0:T(8,128)(2,1)} %all-gather.2.cloned.1.call-done, bf16[1,7168,512]{2,1,0:T(8,128)(2,1)} %param.17), kind=kOutput, calls=%fused_computation.24 | convolution fusion | flops 1879048192 | bytes 11534336 | tf_op jit(solution)/shard_map/dot_general | solution.py:86
  149.5 0.0 copy-start.1
  149.5 0.0 copy-start
  149.6 12.1 %fusion.13 = bf16[256,7168]{1,0:T(8,128)(2,1)} fusion(bf16[1,512,7168]{2,1,0:T(8,128)(2,1)} %param.19, f32[256]{0:T(256)S(1)} %select_reduce_fusion, bf16[256,7168]{1,0:T(8,128)(2,1)} %all-gather.2.cloned.1.call-done, bf16[1,7168,512]{2,1,0:T(8,128)(2,1)} %param.18, f32[256,512]{1,0:T(8,128)S(1)} %fusion.17), kind=kOutput, calls=%fused_computation.20 | convolution fusion | flops 3762552832 | bytes 22545408 | tf_op jit(solution)/shard_map/dot_general | solution.py:89
  161.7 0.0 reduce-scatter.2.cloned.1.call-update
  161.7 0.0 copy-done.1
  161.7 0.6 dynamic_slice.6
  162.9 0.0 copy-done
  162.9 0.2 copy.11
  163.1 3.8 %while.14 = (s32[]{:T(128)}, f32[128]{0:T(128)S(1)}, f32[128]{0:T(128)S(1)}, f32[128,512]{1,0:T(8,128)S(1)}, s32[]{:T(128)}, /*index=5*/s32[]{:T(128)}, bf16[409...) while((s32[]{:T(128)}, f32[128]{0:T(128)S(1)}, ...), condition=%wide.region_3.4_spmd, body=%wide.region_0.3_spmd.sunk | while | flops 143394304 | bytes 2581683 | solution.py:58
  163.1 0.6 add_compare_fusion.2
  163.7 1.5 fusion.48
  165.2 0.2 fusion.49
  165.3 1.5 fusion.50
  166.9 0.7 fusion.33
  167.6 134.2 %reduce-scatter.2.cloned.1.call-done = bf16[8,7168]{1,0:T(8,128)(2,1)} async-done(((bf16[256,7168]{1,0:T(8,128)(2,1)}), bf16[8,7168]{1,0:T(8,128)(2,1)}) %reduce-scatter.2.cloned.1.call-update) | async-done | bytes 114704 | tf_op jit(solution)/shard_map/reduce_scatter | solution.py:91
  (4 shorter events, 0.0 us)
Async XLA Ops:
  7.2 136.1 %all-gather.2.cloned.1.call-start = ((), (), s32[]{:S(2)}) async-start(), calls=%async_computation.1 | async-start | bytes 3784704 | tf_op jit(solution)/shard_map/all_gather | solution.py:82
  7.9 293.9 %reduce-scatter.2.cloned.1.call-start = ((), (), s32[]{:S(2)}) async-start(), calls=%async_computation.2 | async-start | bytes 3784704 | tf_op jit(solution)/shard_map/reduce_scatter | solution.py:91
  149.5 12.2 %copy-start.1 = (s32[32]{0:T(128)S(1)}, s32[32]{0:T(128)}, u32[]{:S(2)}) copy-start(s32[32]{0:T(128)} %param.13) | copy-start | bytes 388
  149.5 13.3 %copy-start = (bf16[1,128,576]{1,2,0:T(8,128)(2,1)S(1)}, bf16[1,128,576]{1,2,0:T(8,128)(2,1)}, u32[]{:S(2)}) copy-start(bf16[1,128,576]{1,2,0:T(8,128)(2,1)} %param.11) | copy-start | bytes 442372
Sparse Core Ops, SparseCore 0:
  10.8 63.3 all-gather.1
  161.8 139.9 reduce-scatter.1

commit v2 on v1

--- a/solution.py
+++ b/solution.py
@@ -1,6 +1,10 @@
+import functools
+
 import jax
 import jax.numpy as jnp
 from jax import lax
+from jax.experimental import pallas as pl
+from jax.experimental.pallas import tpu as pltpu
 from jax.sharding import PartitionSpec as P
 
 WIDTH = 7168
@@ -56,6 +60,318 @@
         return merge_parts(carry, partial_attend(query_row, key_rows, live_mask))
 
     return lax.fori_loop(0, block_total, block_step, initial)
+
+
+def expert_kernel(
+    dims, expert_total, x_ref, gate_hbm, up_hbm, down_hbm, out_ref,
+    rows_in, rows_out, gate_buf, up_buf, down_buf, act_buf, weight_buf,
+    core_in, first_in, second_in, plane_in,
+    load_sem, z_sem, near_sem, far_sem, core_sem, rcore_sem, rfirst_sem, rsecond_sem, rplane_sem,
+):
+    nz, nx, ny = dims
+    width = down_buf.shape[1]
+    half = width // 2
+    full = rows_in.shape[2]
+    dp, y = lax.axis_index("dp"), lax.axis_index("ep")
+    core, x, z = dp % 2, (dp // 2) % nx, dp // (2 * nx)
+
+    def slot(k, a, b, other=0):
+        c = 1 - core if other else core
+        return ((((z + k) % nz) * nx + (x + a) % nx) * 2 + c) * ny + (y + b) % ny
+
+    def device(k=0, a=0, b=0, other=0):
+        c = 1 - core if other else core
+        return ((((z + k) % nz) * nx + (x + a) % nx) * 2 + c, (y + b) % ny)
+
+    def span(h, top):
+        return pl.ds(0, half) if h == 0 else pl.ds(half, top - half)
+
+    loads = [
+        pltpu.make_async_copy(gate_hbm.at[0], gate_buf, load_sem.at[1]),
+        pltpu.make_async_copy(up_hbm.at[0], up_buf, load_sem.at[2]),
+        pltpu.make_async_copy(down_hbm.at[0], down_buf, load_sem.at[3]),
+    ]
+    mine = pltpu.make_async_copy(x_ref, rows_in.at[slot(0, 0, 0)], load_sem.at[0])
+    mine.start()
+    barrier = pltpu.get_barrier_semaphore()
+    partners = [device(other=1)]
+    partners += [device(k=k) for k in range(1, nz)]
+    partners += [device(a=a) for a in range(1, nx)]
+    partners += [device(b=b) for b in range(1, ny)]
+    for partner in partners:
+        pl.semaphore_signal(barrier, inc=1, device_id=partner, device_id_type=pl.DeviceIdType.MESH)
+    for load in loads:
+        load.start()
+    pl.semaphore_wait(barrier, len(partners))
+    mine.wait()
+
+    def remote(src, dst, sems, index, target):
+        return pltpu.make_async_remote_copy(
+            src_ref=src,
+            dst_ref=dst,
+            send_sem=sems.at[(0,) + index],
+            recv_sem=sems.at[(1,) + index],
+            device_id=target,
+            device_id_type=pl.DeviceIdType.MESH,
+        )
+
+    sent = []
+
+    def send(copy):
+        copy.start()
+        sent.append(copy)
+
+    def block_copy(source, h, sems, index, target):
+        part = rows_in.at[source, :, span(h, full)]
+        return remote(part, part, sems, index, target)
+
+    def to_core(k, a, b, h):
+        send(block_copy(slot(-k, -a, -b), h, core_sem, (k, a, b, h), device(other=1)))
+
+    for h in range(2):
+        for k in range(nz - 1, 0, -1):
+            send(block_copy(slot(0, 0, 0), h, z_sem, (k, h), device(k=k)))
+
+    axes = {0: (nx, ny), 1: (ny, nx)}
+
+    def turn(h, first, second):
+        return (first, second) if h == 0 else (second, first)
+
+    def near(k, h, way, hop):
+        a, b = turn(h, hop, 0) if way == 0 else turn(h, 0, hop)
+        return block_copy(slot(-k, 0, 0), h, near_sem, (k, h, way, hop), device(a=a, b=b))
+
+    def far(k, h, i, hop):
+        a, b = turn(h, 0, hop)
+        sa, sb = turn(h, i, 0)
+        return block_copy(slot(-k, -sa, -sb), h, far_sem, (k, h, i, hop), device(a=a, b=b))
+
+    def stage_a(k):
+        for h in range(2):
+            if k > 0:
+                block_copy(slot(-k, 0, 0), h, z_sem, (k, h), device(k=k)).wait_recv()
+            for way in range(2):
+                for hop in range(1, axes[h][way]):
+                    send(near(k, h, way, hop))
+            to_core(k, 0, 0, h)
+
+    def arrived(k, a, b, h, sems, index):
+        block_copy(slot(-k, -a, -b), h, sems, index, device(other=1)).wait_recv()
+
+    def stage_b(k):
+        for h in range(2):
+            for i in range(1, axes[h][0]):
+                a, b = turn(h, i, 0)
+                arrived(k, a, b, h, near_sem, (k, h, 0, i))
+                for hop in range(1, axes[h][1]):
+                    send(far(k, h, i, hop))
+                to_core(k, a, b, h)
+
+    def stage_c(k):
+        for h in range(2):
+            for hop in range(1, axes[h][1]):
+                a, b = turn(h, 0, hop)
+                arrived(k, a, b, h, near_sem, (k, h, 1, hop))
+                to_core(k, a, b, h)
+                for i in range(1, axes[h][0]):
+                    a, b = turn(h, i, hop)
+                    arrived(k, a, b, h, far_sem, (k, h, i, hop))
+                    to_core(k, a, b, h)
+
+    for step in range(nz + 2):
+        if step < nz:
+            stage_a(step)
+        if 0 <= step - 1 < nz:
+            stage_b(step - 1)
+        if 0 <= step - 2 < nz:
+            stage_c(step - 2)
+    for k in range(nz):
+        for a in range(nx):
+            for b in range(ny):
+                for h in range(2):
+                    block_copy(
+                        slot(-k, -a, -b, 1), h, core_sem, (k, a, b, h), device(other=1)
+                    ).wait_recv()
+    loads[0].wait()
+    loads[1].wait()
+    count, rows = rows_in.shape[0], rows_in.shape[1]
+    total = count * rows
+    hidden_units = gate_buf.shape[1]
+    depth = 1024
+    act_buf[...] = jnp.zeros_like(act_buf)
+
+    @pl.loop(0, width // depth)
+    def _(step):
+        cols = pl.ds(pl.multiple_of(step * depth, depth), depth)
+        lhs = rows_in[:, :, cols].astype(jnp.float32).reshape(total, depth).astype(jnp.bfloat16)
+        act_buf[0] += jnp.dot(lhs, gate_buf[cols, :], preferred_element_type=jnp.float32)
+        act_buf[1] += jnp.dot(lhs, up_buf[cols, :], preferred_element_type=jnp.float32)
+
+    coded = rows_in[:, :, width:].astype(jnp.float32).reshape(total, full - width)
+    lane = lax.broadcasted_iota(jnp.int32, coded.shape, 1)
+    chosen = (lane == dp) | (lane == dp + expert_total) | (lane == dp + 2 * expert_total)
+    weight_buf[...] = jnp.sum(jnp.where(chosen, coded, 0.0), axis=1, keepdims=True)
+    gate_act = act_buf[0]
+    hidden = (gate_act / (1.0 + jnp.exp(-gate_act)) * act_buf[1]).astype(jnp.bfloat16)
+    loads[2].wait()
+    piece = 512
+    for h in range(2):
+
+        @pl.loop(0, half // piece)
+        def _(step, h=h):
+            cols = pl.ds(pl.multiple_of(h * half + step * piece, piece), piece)
+            product = jnp.dot(hidden, down_buf[:, cols], preferred_element_type=jnp.float32)
+            product = product * weight_buf[...]
+            rows_out[:, :, cols] = product.reshape(count, rows, piece).astype(jnp.bfloat16)
+
+        for k in list(range(1, nz)) + [0]:
+            for a in range(nx):
+                for b in range(ny):
+                    send(
+                        remote(
+                            rows_out.at[slot(k, a, b, 1), :, span(h, width)],
+                            core_in.at[(k * nx + a) * ny + b, :, span(h, width)],
+                            rcore_sem,
+                            (k, a, b, h),
+                            device(other=1),
+                        )
+                    )
+
+    def add_into(target, h, landed):
+        value = rows_out[target, :, span(h, width)].astype(jnp.float32)
+        for piece_ref in landed:
+            value = value + piece_ref[...].astype(jnp.float32)
+        rows_out[target, :, span(h, width)] = value.astype(jnp.bfloat16)
+
+    most = max(nx, ny)
+
+    def first_copy(k, h, i, hop):
+        a, b = turn(h, i, hop)
+        da, db = turn(h, 0, hop)
+        return remote(
+            rows_out.at[slot(k, a, b), :, span(h, width)],
+            first_in.at[h, (k * most + i) * most + hop],
+            rfirst_sem, (k, h, i, hop), device(a=da, b=db),
+        )
+
+    def second_copy(k, h, i):
+        a, b = turn(h, i, 0)
+        return remote(
+            rows_out.at[slot(k, a, b), :, span(h, width)],
+            second_in.at[h, k * most + i],
+            rsecond_sem, (k, h, i), device(a=a, b=b),
+        )
+
+    def plane_copy(k, h):
+        return remote(
+            rows_out.at[slot(k, 0, 0), :, span(h, width)],
+            plane_in.at[k, :, span(h, width)],
+            rplane_sem, (k, h), device(k=k),
+        )
+
+    def back_a(k):
+        for h in range(2):
+            for hop in list(range(1, axes[h][1])) + [0]:
+                for i in range(axes[h][0]):
+                    a, b = turn(h, i, hop)
+                    landed = core_in.at[(k * nx + a) * ny + b, :, span(h, width)]
+                    remote(landed, landed, rcore_sem, (k, a, b, h), device(other=1)).wait_recv()
+                    add_into(slot(k, a, b), h, [landed])
+                    if hop > 0:
+                        send(first_copy(k, h, i, hop))
+
+    def back_b(k):
+        for h in range(2):
+            for i in list(range(1, axes[h][0])) + [0]:
+                a, b = turn(h, i, 0)
+                landed = []
+                for hop in range(1, axes[h][1]):
+                    first_copy(k, h, i, hop).wait_recv()
+                    landed.append(first_in.at[h, (k * most + i) * most + hop])
+                add_into(slot(k, a, b), h, landed)
+                if i > 0:
+                    send(second_copy(k, h, i))
+
+    def back_c(k):
+        for h in range(2):
+            landed = []
+            for i in range(1, axes[h][0]):
+                second_copy(k, h, i).wait_recv()
+                landed.append(second_in.at[h, k * most + i])
+            add_into(slot(k, 0, 0), h, landed)
+            if k > 0:
+                send(plane_copy(k, h))
+
+    order = list(range(1, nz)) + [0]
+    for step in range(nz + 2):
+        if step < nz:
+            back_a(order[step])
+        if 0 <= step - 1 < nz:
+            back_b(order[step - 1])
+        if 0 <= step - 2 < nz:
+            back_c(order[step - 2])
+    for h in range(2):
+        value = rows_out[slot(0, 0, 0), :, span(h, width)].astype(jnp.float32)
+        for k in range(1, nz):
+            plane_copy(k, h).wait_recv()
+            value = value + plane_in[k, :, span(h, width)].astype(jnp.float32)
+        out_ref[:, span(h, width)] = value.astype(jnp.bfloat16)
+    for copy in sent:
+        copy.wait_send()
+
+
+def expert_layer(moe_input, expert_ids, gate_weights, expert_gate, expert_up, expert_down):
+    ranks_dp, ranks_ep = lax.axis_size("dp"), lax.axis_size("ep")
+    nx = ranks_ep if ranks_dp % (2 * ranks_ep) == 0 else 1
+    dims = (ranks_dp // (2 * nx), nx, ranks_ep)
+    nz, ny, most = dims[0], dims[2], max(nx, ranks_ep)
+    rows, width = moe_input.shape
+    ranks_all = ranks_dp * ranks_ep
+    half = width // 2
+    named = expert_ids[:, :, None] == jnp.arange(ranks_dp, dtype=jnp.int32)[None, None, :]
+    table = jnp.sum(jnp.where(named, gate_weights[:, :, None], 0.0), axis=1)
+    high = lax.reduce_precision(table, 8, 7)
+    middle = lax.reduce_precision(table - high, 8, 7)
+    low = table - high - middle
+    pad = -3 * ranks_dp % 128
+    coded = jnp.pad(jnp.concatenate([high, middle, low], axis=1), ((0, 0), (0, pad)))
+    block = jnp.concatenate([moe_input, coded.astype(jnp.bfloat16)], axis=1)
+    full = block.shape[1]
+    units = expert_gate.shape[2]
+    dma = pltpu.SemaphoreType.DMA
+    bf16, f32 = jnp.bfloat16, jnp.float32
+    anywhere = pl.BlockSpec(memory_space=pl.ANY)
+    return pl.pallas_call(
+        functools.partial(expert_kernel, dims, ranks_dp),
+        out_shape=jax.ShapeDtypeStruct((rows, width), bf16),
+        in_specs=[anywhere] * 4,
+        out_specs=pl.BlockSpec(memory_space=pltpu.VMEM),
+        scratch_shapes=[
+            pltpu.VMEM((ranks_all, rows, full), bf16),
+            pltpu.VMEM((ranks_all, rows, width), bf16),
+            pltpu.VMEM((width, units), bf16),
+            pltpu.VMEM((width, units), bf16),
+            pltpu.VMEM((units, width), bf16),
+            pltpu.VMEM((2, ranks_all * rows, units), f32),
+            pltpu.VMEM((ranks_all * rows, 1), f32),
+            pltpu.VMEM((ranks_all // 2, rows, width), bf16),
+            pltpu.VMEM((2, nz * most * most, rows, half), bf16),
+            pltpu.VMEM((2, nz * most, rows, half), bf16),
+            pltpu.VMEM((nz, rows, width), bf16),
+            dma((4,)),
+            dma((2, nz, 2)),
+            dma((2, nz, 2, 2, most)),
+            dma((2, nz, 2, most, most)),
+            dma((2, nz, nx, ny, 2)),
+            dma((2, nz, nx, ny, 2)),
+            dma((2, nz, 2, most, most)),
+            dma((2, nz, 2, most)),
+            dma((2, nz, 2)),
+        ],
+        compiler_params=pltpu.CompilerParams(
+            collective_id=0, has_side_effects=True, vmem_limit_bytes=63 * 1024 * 1024
+        ),
+    )(block, expert_gate, expert_up, expert_down)
 
 
 def per_device(
@@ -78,18 +394,10 @@
     query_row = query_rows[0]
     score_top, weight_sum, mixed_values = local_attend(query_row, cache_latent, own_length)
     attn_out = (mixed_values / weight_sum[:, None]).astype(jnp.bfloat16)[None]
-    axes = ("dp", "ep")
-    all_rows = lax.all_gather(moe_input, axes, axis=0, tiled=True)
-    all_ids = lax.all_gather(expert_ids, axes, axis=0, tiled=True)
-    all_weights = lax.all_gather(gate_weights, axes, axis=0, tiled=True)
-    row_weight = jnp.sum(jnp.where(all_ids == here_dp, all_weights, 0.0), axis=1, keepdims=True)
-    gate_act = jnp.dot(all_rows, expert_gate[0], preferred_element_type=jnp.float32)
-    up_act = jnp.dot(all_rows, expert_up[0], preferred_element_type=jnp.float32)
-    hidden = (jax.nn.silu(gate_act) * up_act).astype(jnp.bfloat16)
-    partial_sum = jnp.dot(hidden, expert_down[0], preferred_element_type=jnp.float32)
-    weighted = (partial_sum * row_weight).astype(jnp.bfloat16)
-    moe_sum = lax.psum_scatter(weighted, axes, scatter_dimension=0, tiled=True)
-    return (attn_out, moe_sum.astype(jnp.bfloat16))
+    moe_out = expert_layer(
+        moe_input, expert_ids, gate_weights, expert_gate, expert_up, expert_down
+    )
+    return (attn_out, moe_out)
 
 
 def solution(mesh):

time: 310 us -> 99.6 us (0.32)
  blocking collectives: 135 us -> 0 us
  waiting for transfers between devices: 135 us -> 0 us
  Pallas kernels: 0 us -> 87.2 us
  matrix products: 21.3 us -> 2.98 us
  between operations: 14.7 us -> 1.39 us
  local copies, waits for them, and re-layouts: 0.79 us -> 3.9 us
    all_gather x2 -> x0, blocking collectives: 135 us -> none  [the longest x1 70.9 us: per_device(): all_ids = lax.all_gather(expert_ids, axes, axis=0, tiled=True)]
    reduce_scatter x1 -> x0, waiting for transfers between devices: 134 us -> none  [per_device(): moe_sum = lax.psum_scatter(weighted, axes, scatter_dimension=0, tiled=True)]
    pallas_call x0 -> x1, Pallas kernels: none -> 87.2 us  [expert_layer(): pl.pallas_call(functools.partial(expert_kernel, dims, ranks_dp), out_shap...]
    dot_general x2 -> x0, matrix products: 18.4 us -> none  [the longest x1 12.1 us: per_device(): jnp.dot(hidden, expert_down[0], preferred_element_type=jnp.float32)]
  transfers between devices with their start and end apart: 2 -> 0, of which waited for: 1 -> 0; matrix products, arithmetic and copies ran while one was open for 2% -> 0% of each run, Pallas kernels for 0% -> 0%
where the time goes in v2:
time: 99.6 us; the launch traced here: 98 us
  Pallas kernels  87.2 us (88%)
  local copies, waits for them, and re-layouts  3.9 us (4%)
  matrix products  2.98 us (3%)
  other arithmetic  2.44 us (2%)
  between operations  1.39 us (1%)
    pallas_call x1, Pallas kernels, expert_layer(): pl.pallas_call(functools.partial(expert_kernel, dims, ranks_dp), out_shap...  87.2 us
    unnamed x8, local copies, waits for them, and re-layouts  2.63 us

profile of v2, /device:TPU:0, one launch (start us, length us, event | category | flops | bytes accessed | tf_op | source)
XLA Modules:
  0.0 98.0 jit_solution(16706044646438316708)
XLA Ops:
  0.6 1.2 %dynamic_slice.6 = s32[1]{0:T(128)} dynamic-slice(s32[32]{0:T(128)} %param.13, s32[]{:T(128)S(6)} %select_n.23), dynamic_slice_sizes={1} | dynamic-slice | bytes 12 | tf_op jit(solution)/shard_map/dynamic_slice | solution.py:393
  2.5 1.1 %copy.12 = bf16[1,128,576]{2,1,0:T(8,128)(2,1)S(1)} copy(bf16[1,128,576]{1,2,0:T(8,128)(2,1)} %param.11) | data formatting | bytes 294912 | tf_op args[0]
  3.7 0.0 copy-start.1
  3.7 0.0 copy-start.2
  3.7 0.0 copy-start
  3.7 3.9 %while.14 = (s32[]{:T(128)}, f32[128]{0:T(128)S(1)}, f32[128]{0:T(128)S(1)}, f32[128,512]{1,0:T(8,128)S(1)}, s32[]{:T(128)}, /*index=5*/s32[]{:T(128)}, bf16[409...) while((s32[]{:T(128)}, f32[128]{0:T(128)S(1)}, ...), condition=%wide.region_3.4_spmd, body=%wide.region_0.3_spmd.sunk | while | flops 143394304 | bytes 2581691 | solution.py:62
  3.7 0.7 add_compare_fusion.2
  4.4 1.5 %fusion.31 = (f32[128]{0:T(128)S(1)}, f32[512,128]{1,0:T(8,128)S(1)}) fusion(bf16[128,576]{1,0:T(8,128)(2,1)S(1)} %get-tuple-element.166, bf16[4096,576]{0,1:T(8,128)(2,1)} %get-tuple-element.165, s32[]{:T(128)S(6)} %select_n.40, pred[512]{0:T(512)(128)(4,1)S(1)} %add_compare_fusion.2), kind=kOutput, calls=%fused_computation.35.clone.1 | convolution fusion | flops 75693952 | bytes 1000452 | tf_op jit(solution)/shard_map/while/body/dot_general | solution.py:21
  5.9 0.2 fusion.32
  6.1 1.5 %fusion.33 = f32[128,512]{1,0:T(8,128)S(1)} fusion(bf16[4096,576]{0,1:T(8,128)(2,1)} %get-tuple-element.165, s32[]{:T(128)S(6)} %select_n.40, f32[128,512]{1,0:T(8,128)S(1)} %get-tuple-element.150, f32[512,128]{1,0:T(8,128)S(1)} %get-tuple-element.129, f32[128]{0:T(128)S(1)} %get-tuple-element.133, f32[128]{0:T(128)S(1)} %get-tuple-element.134, ...), kind=kOutput, calls=%fused_computation.2.clone.1 | convolution fusion | flops 67502080 | bytes 1312772 | tf_op jit(solution)/shard_map/while/body/dot_general | solution.py:28
  7.6 0.7 fusion.13
  8.3 0.0 copy-done.1
  8.3 0.0 copy-done.2
  8.3 0.1 select_reduce_fusion
  8.5 0.1 fusion.19
  8.5 0.0 copy-done
  8.5 0.6 pad_maximum_fusion.x_ref
  9.2 87.2 %shard_map.104 = bf16[8,7168]{1,0:T(8,128)(2,1)} custom-call(bf16[8,7296]{1,0:T(8,128)(2,1)} %pad_maximum_fusion.x_ref, bf16[1,7168,512]{2,1,0:T(8,128)(2,1)} %gate_hbm.1, bf16[1,7168,512]{2,1,0:T(8,128)(2,1)} %up_hbm.1, bf16[1,512,7168]{2,1,0:T(8,128)(2,1)} %down_hbm.1), custom_call_target="tpu_custom_call" | custom-call | tf_op jit(solution)/shard_map/pallas_call | solution.py:344
  96.4 1.6 %copy.26 = bf16[8,7168]{1,0:T(8,128)(2,1)} copy(bf16[8,7168]{1,0:T(8,128)(2,1)} %shard_map.104) | data formatting | bytes 229376
  (5 shorter events, 0.1 us)
Async XLA Ops:
  3.7 4.7 %copy-start.1 = (f32[8,8]{1,0:T(8,128)S(1)}, f32[8,8]{1,0:T(8,128)}, u32[]{:S(2)}) copy-start(f32[8,8]{1,0:T(8,128)} %param.16) | copy-start | bytes 772
  3.7 4.7 %copy-start.2 = (s32[8,8]{1,0:T(8,128)S(1)}, s32[8,8]{1,0:T(8,128)}, u32[]{:S(2)}) copy-start(s32[8,8]{1,0:T(8,128)} %param.15) | copy-start | bytes 772
  3.7 4.9 %copy-start = (bf16[8,7168]{1,0:T(8,128)(2,1)S(1)}, bf16[8,7168]{1,0:T(8,128)(2,1)}, u32[]{:S(2)}) copy-start(bf16[8,7168]{1,0:T(8,128)(2,1)} %param.14) | copy-start | bytes 344068

commit v3 on v2

--- a/solution.py
+++ b/solution.py
@@ -9,61 +9,15 @@
 
 WIDTH = 7168
 LATENT = 512
-TOPK = 8
-
 
 qk_scale = 192.0 ** (-0.5)
 far_low = -1e30
 attend_rows = 512
 
 
-def partial_attend(query_row, key_rows, live_mask):
-    scores = qk_scale * lax.dot_general(
-        query_row, key_rows, (((1,), (1,)), ((), ())), preferred_element_type=jnp.float32
-    )
-    scores = jnp.where(live_mask[None, :], scores, far_low)
-    score_top = jnp.max(scores, axis=1)
-    exponent = jnp.where(live_mask[None, :], jnp.exp(scores - score_top[:, None]), 0.0)
-    weight_sum = jnp.sum(exponent, axis=1)
-    mixed_values = jnp.dot(
-        exponent.astype(jnp.bfloat16), key_rows[:, :LATENT], preferred_element_type=jnp.float32
-    )
-    return (score_top, weight_sum, mixed_values)
-
-
-def merge_parts(first, second):
-    top_first, sum_first, mix_first = first
-    top_second, sum_second, mix_second = second
-    score_top = jnp.maximum(top_first, top_second)
-    scale_first = jnp.exp(top_first - score_top)
-    scale_second = jnp.exp(top_second - score_top)
-    return (
-        score_top,
-        sum_first * scale_first + sum_second * scale_second,
-        mix_first * scale_first[:, None] + mix_second * scale_second[:, None],
-    )
-
-
-def local_attend(query_row, cache_rows, keep_end):
-    head_count = query_row.shape[0]
-    block_total = (keep_end + attend_rows - 1) // attend_rows
-    initial = (
-        jnp.full((head_count,), far_low, jnp.float32),
-        jnp.zeros((head_count,), jnp.float32),
-        jnp.zeros((head_count, LATENT), jnp.float32),
-    )
-
-    def block_step(block_index, carry):
-        start_row = block_index * attend_rows
-        key_rows = lax.dynamic_slice_in_dim(cache_rows, start_row, attend_rows, 0)
-        live_mask = start_row + jnp.arange(attend_rows, dtype=jnp.int32) < keep_end
-        return merge_parts(carry, partial_attend(query_row, key_rows, live_mask))
-
-    return lax.fori_loop(0, block_total, block_step, initial)
-
-
-def expert_kernel(
-    dims, expert_total, x_ref, gate_hbm, up_hbm, down_hbm, out_ref,
+def joint_kernel(
+    dims, expert_total, length_ref, query_ref, cache_hbm, x_ref, gate_hbm, up_hbm, down_hbm,
+    attn_ref, out_ref, cache_buf, mixed_buf, sum_buf, top_buf,
     rows_in, rows_out, gate_buf, up_buf, down_buf, act_buf, weight_buf,
     core_in, first_in, second_in, plane_in,
     load_sem, z_sem, near_sem, far_sem, core_sem, rcore_sem, rfirst_sem, rsecond_sem, rplane_sem,
@@ -86,6 +40,7 @@
     def span(h, top):
         return pl.ds(0, half) if h == 0 else pl.ds(half, top - half)
 
+    cache_load = pltpu.make_async_copy(cache_hbm, cache_buf, load_sem.at[4])
     loads = [
         pltpu.make_async_copy(gate_hbm.at[0], gate_buf, load_sem.at[1]),
         pltpu.make_async_copy(up_hbm.at[0], up_buf, load_sem.at[2]),
@@ -100,6 +55,7 @@
     partners += [device(b=b) for b in range(1, ny)]
     for partner in partners:
         pl.semaphore_signal(barrier, inc=1, device_id=partner, device_id_type=pl.DeviceIdType.MESH)
+    cache_load.start()
     for load in loads:
         load.start()
     pl.semaphore_wait(barrier, len(partners))
@@ -128,8 +84,8 @@
     def to_core(k, a, b, h):
         send(block_copy(slot(-k, -a, -b), h, core_sem, (k, a, b, h), device(other=1)))
 
-    for h in range(2):
-        for k in range(nz - 1, 0, -1):
+    for k in range(1, nz):
+        for h in range(2):
             send(block_copy(slot(0, 0, 0), h, z_sem, (k, h), device(k=k)))
 
     axes = {0: (nx, ny), 1: (ny, nx)}
@@ -178,13 +134,56 @@
                     arrived(k, a, b, h, far_sem, (k, h, i, hop))
                     to_core(k, a, b, h)
 
+    blocks = cache_buf.shape[1] // attend_rows
+    length = length_ref[dp * ny + y]
+    query = query_ref[0].T
+
+    def attend_block(block):
+        keys = cache_buf[:, block * attend_rows : (block + 1) * attend_rows]
+        place = lax.broadcasted_iota(jnp.int32, (1, attend_rows), 1) + block * attend_rows
+        scores = qk_scale * jnp.dot(query, keys, preferred_element_type=jnp.float32)
+        scores = jnp.where(place < length, scores, far_low)
+        top = jnp.max(scores, axis=1, keepdims=True)
+        if block > 0:
+            top = jnp.maximum(top_buf[...], top)
+        exponent = jnp.where(place < length, jnp.exp(scores - top), 0.0)
+        weight = jnp.sum(exponent, axis=1, keepdims=True)
+        mixed = lax.dot_general(
+            exponent.astype(jnp.bfloat16),
+            keys[:LATENT],
+            (((1,), (1,)), ((), ())),
+            preferred_element_type=jnp.float32,
+        )
+        if block > 0:
+            scale = jnp.exp(top_buf[...] - top)
+            weight = weight + sum_buf[...] * scale
+            mixed = mixed + mixed_buf[...] * scale
+        top_buf[...] = top
+        sum_buf[...] = weight
+        mixed_buf[...] = mixed
+
+    units = [functools.partial(attend_block, block) for block in range(blocks)][::-1]
+
+    def attend(number):
+        for _ in range(min(number, len(units))):
+            units.pop()()
+
     for step in range(nz + 2):
         if step < nz:
             stage_a(step)
+        if step == 0:
+            cache_load.wait()
+            attend(2)
+        else:
+            attend(1)
         if 0 <= step - 1 < nz:
             stage_b(step - 1)
+            attend(1)
         if 0 <= step - 2 < nz:
             stage_c(step - 2)
+            attend(1)
+    attend(len(units))
+    attn_ref[0] = mixed_buf[...] / sum_buf[...]
     for k in range(nz):
         for a in range(nx):
             for b in range(ny):
@@ -250,7 +249,7 @@
         da, db = turn(h, 0, hop)
         return remote(
             rows_out.at[slot(k, a, b), :, span(h, width)],
-            first_in.at[h, (k * most + i) * most + hop],
+            first_in.at[h, (k * most + i) * (most - 1) + hop - 1],
             rfirst_sem, (k, h, i, hop), device(a=da, b=db),
         )
 
@@ -258,14 +257,14 @@
         a, b = turn(h, i, 0)
         return remote(
             rows_out.at[slot(k, a, b), :, span(h, width)],
-            second_in.at[h, k * most + i],
+            second_in.at[h, k * (most - 1) + i - 1],
             rsecond_sem, (k, h, i), device(a=a, b=b),
         )
 
     def plane_copy(k, h):
         return remote(
             rows_out.at[slot(k, 0, 0), :, span(h, width)],
-            plane_in.at[k, :, span(h, width)],
+            plane_in.at[k - 1, :, span(h, width)],
             rplane_sem, (k, h), device(k=k),
         )
 
@@ -287,7 +286,7 @@
                 landed = []
                 for hop in range(1, axes[h][1]):
                     first_copy(k, h, i, hop).wait_recv()
-                    landed.append(first_in.at[h, (k * most + i) * most + hop])
+                    landed.append(first_in.at[h, (k * most + i) * (most - 1) + hop - 1])
                 add_into(slot(k, a, b), h, landed)
                 if i > 0:
                     send(second_copy(k, h, i))
@@ -297,7 +296,7 @@
             landed = []
             for i in range(1, axes[h][0]):
                 second_copy(k, h, i).wait_recv()
-                landed.append(second_in.at[h, k * most + i])
+                landed.append(second_in.at[h, k * (most - 1) + i - 1])
             add_into(slot(k, 0, 0), h, landed)
             if k > 0:
                 send(plane_copy(k, h))
@@ -314,13 +313,13 @@
         value = rows_out[slot(0, 0, 0), :, span(h, width)].astype(jnp.float32)
         for k in range(1, nz):
             plane_copy(k, h).wait_recv()
-            value = value + plane_in[k, :, span(h, width)].astype(jnp.float32)
-        out_ref[:, span(h, width)] = value.astype(jnp.bfloat16)
+            value = value + plane_in[k - 1, :, span(h, width)].astype(jnp.float32)
+        out_ref[:, span(h, width)] = value
     for copy in sent:
         copy.wait_send()
 
 
-def expert_layer(moe_input, expert_ids, gate_weights, expert_gate, expert_up, expert_down):
+def both_layers(lengths, query_rows, cache_latent, moe_input, expert_ids, gate_weights, expert_gate, expert_up, expert_down):
     ranks_dp, ranks_ep = lax.axis_size("dp"), lax.axis_size("ep")
     nx = ranks_ep if ranks_dp % (2 * ranks_ep) == 0 else 1
     dims = (ranks_dp // (2 * nx), nx, ranks_ep)
@@ -341,12 +340,24 @@
     dma = pltpu.SemaphoreType.DMA
     bf16, f32 = jnp.bfloat16, jnp.float32
     anywhere = pl.BlockSpec(memory_space=pl.ANY)
+    heads = query_rows.shape[2]
     return pl.pallas_call(
-        functools.partial(expert_kernel, dims, ranks_dp),
-        out_shape=jax.ShapeDtypeStruct((rows, width), bf16),
-        in_specs=[anywhere] * 4,
-        out_specs=pl.BlockSpec(memory_space=pltpu.VMEM),
+        functools.partial(joint_kernel, dims, ranks_dp),
+        out_shape=(
+            jax.ShapeDtypeStruct((1, heads, LATENT), f32),
+            jax.ShapeDtypeStruct((rows, width), f32),
+        ),
+        in_specs=[
+            pl.BlockSpec(memory_space=pltpu.SMEM),
+            pl.BlockSpec(memory_space=pltpu.VMEM),
+        ]
+        + [anywhere] * 5,
+        out_specs=(pl.BlockSpec(memory_space=pltpu.VMEM),) * 2,
         scratch_shapes=[
+            pltpu.VMEM(cache_latent.shape, bf16),
+            pltpu.VMEM((heads, LATENT), f32),
+            pltpu.VMEM((heads, 1), f32),
+            pltpu.VMEM((heads, 1), f32),
             pltpu.VMEM((ranks_all, rows, full), bf16),
             pltpu.VMEM((ranks_all, rows, width), bf16),
             pltpu.VMEM((width, units), bf16),
@@ -355,10 +366,10 @@
             pltpu.VMEM((2, ranks_all * rows, units), f32),
             pltpu.VMEM((ranks_all * rows, 1), f32),
             pltpu.VMEM((ranks_all // 2, rows, width), bf16),
-            pltpu.VMEM((2, nz * most * most, rows, half), bf16),
-            pltpu.VMEM((2, nz * most, rows, half), bf16),
-            pltpu.VMEM((nz, rows, width), bf16),
-            dma((4,)),
+            pltpu.VMEM((2, nz * most * max(most - 1, 1), rows, half), bf16),
+            pltpu.VMEM((2, nz * max(most - 1, 1), rows, half), bf16),
+            pltpu.VMEM((max(nz - 1, 1), rows, width), bf16),
+            dma((5,)),
             dma((2, nz, 2)),
             dma((2, nz, 2, 2, most)),
             dma((2, nz, 2, most, most)),
@@ -369,9 +380,9 @@
             dma((2, nz, 2)),
         ],
         compiler_params=pltpu.CompilerParams(
-            collective_id=0, has_side_effects=True, vmem_limit_bytes=63 * 1024 * 1024
+            collective_id=0, has_side_effects=True, vmem_limit_bytes=67043328
         ),
-    )(block, expert_gate, expert_up, expert_down)
+    )(lengths, query_rows, cache_latent, block, expert_gate, expert_up, expert_down)
 
 
 def per_device(
@@ -385,19 +396,11 @@
     expert_up,
     expert_down,
 ):
-    ranks_dp = lax.axis_size("dp")
-    ranks_ep = lax.axis_size("ep")
-    here_dp = lax.axis_index("dp")
-    here_ep = lax.axis_index("ep")
-    own_rank = here_dp * ranks_ep + here_ep
-    own_length = lengths[own_rank]
-    query_row = query_rows[0]
-    score_top, weight_sum, mixed_values = local_attend(query_row, cache_latent, own_length)
-    attn_out = (mixed_values / weight_sum[:, None]).astype(jnp.bfloat16)[None]
-    moe_out = expert_layer(
-        moe_input, expert_ids, gate_weights, expert_gate, expert_up, expert_down
+    attn_out, moe_out = both_layers(
+        lengths, jnp.swapaxes(query_rows, 1, 2), cache_latent.T, moe_input, expert_ids,
+        gate_weights, expert_gate, expert_up, expert_down,
     )
-    return (attn_out, moe_out)
+    return attn_out.astype(jnp.bfloat16), moe_out.astype(jnp.bfloat16)
 
 
 def solution(mesh):

time: 99.6 us -> 70.6 us (0.71); the launches traced: 98 us -> 70.3 us
  Pallas kernels: 87.2 us -> 64 us
  local copies, waits for them, and re-layouts: 3.9 us -> 0 us
  other arithmetic: 2.44 us -> 5.65 us
  matrix products: 2.98 us -> 0 us
    pallas_call x1, Pallas kernels: 87.2 us -> 64 us  [both_layers(): pl.pallas_call(functools.partial(joint_kernel, dims, ranks_dp), out_shape...]
    convert_element_type x0 -> x2, other arithmetic: none -> 3.22 us  [per_device(): return (attn_out.astype(jnp.bfloat16), moe_out.astype(jnp.bfloat16))]
    dot_general x2 -> x0, matrix products: 2.98 us -> none  [the longest x1 1.52 us: partial_attend(): jnp.dot(exponent.astype(jnp.bfloat16), key_rows[:, :LATENT], preferred_el...]
    unnamed x8 -> x0, local copies, waits for them, and re-layouts: 2.63 us -> none
    dynamic_slice x1 -> x0, local copies, waits for them, and re-layouts: 1.24 us -> none  [per_device(): own_length = lengths[own_rank]]
where the time goes in v3:
time: 70.6 us; the launch traced here: 70.3 us
  Pallas kernels  64 us (91%)
  other arithmetic  5.65 us (8%)
    pallas_call x1, Pallas kernels, both_layers(): pl.pallas_call(functools.partial(joint_kernel, dims, ranks_dp), out_shape...  64 us
    convert_element_type x2, other arithmetic, per_device(): return (attn_out.astype(jnp.bfloat16), moe_out.astype(jnp.bfloat16))  3.22 us
    concatenate x1, other arithmetic, both_layers(): block = jnp.concatenate([moe_input, coded.astype(jnp.bfloat16)], axis=1)  1.55 us

profile of v3, /device:TPU:0, one launch (start us, length us, event | category | flops | bytes accessed | tf_op | source)
XLA Modules:
  0.0 70.3 jit_solution(2856910056788398245)
XLA Ops:
  0.6 0.8 %select_reduce_fusion = f32[8,16]{1,0:T(8,128)S(1)} fusion(f32[8,8]{1,0:T(8,128)} %param.14, s32[8,8]{1,0:T(8,128)} %param.13), kind=kLoop, calls=%fused_computation.1 | loop fusion | flops 2944 | bytes 1024 | tf_op jit(solution)/shard_map/reduce_sum | solution.py:331
  1.4 0.1 fusion.5
  1.5 1.6 %pad_maximum_fusion.x_ref = bf16[8,7296]{1,0:T(8,128)(2,1)} fusion(bf16[8,128]{1,0:T(8,128)(2,1)S(1)} %fusion.5, bf16[8,7168]{1,0:T(8,128)(2,1)} %param.12), kind=kLoop, calls=%fused_computation | loop fusion | flops 233472 | bytes 233472 | tf_op jit(solution)/shard_map/concatenate | solution.py:337
  3.1 64.0 %shard_map.104 = (f32[1,128,512]{2,1,0:T(8,128)}, f32[8,7168]{1,0:T(8,128)}) custom-call(s32[32]{0:T(128)} %length_ref.1, bf16[1,576,128]{2,1,0:T(8,128)(2,1)} %bitcast.3, bf16[576,4096]{1,0:T(8,128)(2,1)} %bitcast.2, bf16[8,7296]{1,0:T(8,128)(2,1)} %pad_maximum_fusion.x_ref, bf16[1,7168,512]{2,1,0:T(8,128)(2,1)} %gate_hbm.1, bf16[1,7168,512]{2,1,0:T(8,128)(2,1)} %up_hbm.1, ...), custom_call_target="tpu_custom_call" | custom-call | tf_op jit(solution)/shard_map/pallas_call | solution.py:344
  67.1 1.6 %convert_element_type.9 = bf16[1,128,512]{2,1,0:T(8,128)(2,1)} convert(f32[1,128,512]{2,1,0:T(8,128)} %get-tuple-element.4) | non-fusion elementwise | flops 65536 | bytes 393216 | tf_op jit(solution)/shard_map/convert_element_type | solution.py:403
  68.7 1.6 %convert_element_type.10 = bf16[8,7168]{1,0:T(8,128)(2,1)} convert(f32[8,7168]{1,0:T(8,128)} %get-tuple-element.5) | non-fusion elementwise | flops 57344 | bytes 344064 | tf_op jit(solution)/shard_map/convert_element_type | solution.py:403
  (1 shorter events, 0.0 us)
